TPU v7x, 32 devices: a whole 2x2x4 slice. The times are simulated.
32 devices in a mesh: wide: 8 (over y, x, core), narrow: 4 (over z).
Axes of the slice: x: 2, y: 2, z: 4, core: 2. Of those that a mesh axis runs over, the one named last changes fastest.
Arguments:
- layer_input: bfloat16 [2, 8, 256, 2048], P(None, 'wide', 'narrow'), may hold values from -6 to 6
- document_lengths: int32 [2, 8, 4], P(None, 'wide'), may hold values from 1 to 128, 256 in all within a row
- attn_gain: bfloat16 [2048], replicated, may hold values from 0.5 to 1.5
- w_query: bfloat16 [2048, 2048], P(None, 'narrow'), may hold values from -0.125 to 0.125
- w_key: bfloat16 [2048, 1024], P(None, 'narrow'), may hold values from -0.125 to 0.125
- w_value: bfloat16 [2048, 1024], P(None, 'narrow'), may hold values from -0.125 to 0.125
- query_gain: bfloat16 [128], replicated, may hold values from 1 to 2.5
- key_gain: bfloat16 [128], replicated, may hold values from 1 to 2.5
- w_out: bfloat16 [2048, 2048], P('narrow'), may hold values from -0.75 to 0.75
- mlp_gain: bfloat16 [2048], replicated, may hold values from 0.5 to 1.5
- w_gate: bfloat16 [2048, 6144], P(None, 'narrow'), may hold values from -0.125 to 0.125
- w_up: bfloat16 [2048, 6144], P(None, 'narrow'), may hold values from -0.125 to 0.125
- w_down: bfloat16 [6144, 2048], P('narrow'), may hold values from -0.078125 to 0.078125
- output_cotangent: bfloat16 [2, 8, 256, 2048], P(None, 'wide', 'narrow'), may hold values from -6 to 6
Outputs:
- layer_out: float32 [2, 8, 256, 2048], P(None, 'wide', 'narrow')
- in_grad: float32 [2, 8, 256, 2048], P(None, 'wide', 'narrow')
- attn_gain_grad: float32 [2048], replicated
- w_query_grad: float32 [2048, 2048], P('wide', 'narrow')
- w_key_grad: float32 [2048, 1024], P('wide', 'narrow')
- w_value_grad: float32 [2048, 1024], P('wide', 'narrow')
- query_gain_grad: float32 [128], replicated
- key_gain_grad: float32 [128], replicated
- w_out_grad: float32 [2048, 2048], P('narrow', 'wide')
- mlp_gain_grad: float32 [2048], replicated
- w_gate_grad: float32 [2048, 6144], P('wide', 'narrow')
- w_up_grad: float32 [2048, 6144], P('wide', 'narrow')
- w_down_grad: float32 [6144, 2048], P('narrow', 'wide')
Inputs may be any that keep to these rules, and one draw needn't show every extreme that they name: `document_lengths`: each row's 4 document lengths sum to 256, and in every row the longest is exactly 128.
All inputs are finite; a program needn't handle non-finite values.
Results may differ from a plain program's by a relative error of at most 0.013.
The roundings to bfloat16 on the way count: a program that leaves them out, or rounds other values in their place, can miss the bound.
Values may be sent and summed in bfloat16 or wider, within the bound.
A program may use at most 192 MiB of HBM per device.

v0:
```python
import jax
import jax.numpy as jnp
from jax import lax
from jax.sharding import PartitionSpec as P

norm_eps = 1e-06
masked_score = -1e30


def rms_scale(values):
    return lax.rsqrt(jnp.mean(values * values, axis=-1, keepdims=True) + norm_eps)


def rms_back(grad_in, normed_hat, scale_rows):
    return scale_rows * (
        grad_in - normed_hat * jnp.mean(grad_in * normed_hat, axis=-1, keepdims=True)
    )


def doc_layout(lengths, seq_len):
    doc_ends = jnp.cumsum(lengths)
    starts = doc_ends - lengths
    places = lax.iota(jnp.int32, seq_len)
    segment = jnp.sum((places[:, None] >= doc_ends[None, :]).astype(jnp.int32), axis=1)
    member = segment[:, None] == lax.iota(jnp.int32, lengths.shape[0])[None, :]
    doc_first = jnp.sum(jnp.where(member, starts[None, :], 0), axis=1)
    allowed = (segment[:, None] == segment[None, :]) & (places[None, :] <= places[:, None])
    return (places - doc_first, allowed)


def rope_tables(inside, head_dim):
    half_dim = head_dim // 2
    frequency = jnp.power(1000000.0, -2.0 * lax.iota(jnp.float32, half_dim) / head_dim)
    angles = inside.astype(jnp.float32)[:, None] * frequency[None, :]
    return (jnp.cos(angles), jnp.sin(angles))


def rotate(values, cos_table, sine_table):
    half_dim = values.shape[-1] // 2
    first_half = values[..., :half_dim]
    second = values[..., half_dim:]
    cos_wide = cos_table[:, None, :]
    sine_wide = sine_table[:, None, :]
    return jnp.concatenate(
        [first_half * cos_wide - second * sine_wide, second * cos_wide + first_half * sine_wide],
        axis=-1,
    )


def contract_rows(left_side, right_side):
    return lax.dot_general(
        left_side, right_side, (((0,), (0,)), ((), ())), preferred_element_type=jnp.float32
    )


def contract_cols(left_side, right_side):
    return lax.dot_general(
        left_side, right_side, (((1,), (1,)), ((), ())), preferred_element_type=jnp.float32
    )


def row_product(source, weight):
    return jnp.dot(source, weight, preferred_element_type=jnp.float32)


def row_back_product(source, weight):
    return contract_cols(source, weight)


def attention_scores(grouped, key_rot, allowed, score_scale):
    raw_scores = (
        jnp.einsum("tkgd,ukd->kgtu", grouped, key_rot, preferred_element_type=jnp.float32)
        * score_scale
    )
    return jnp.where(allowed[None, None], raw_scores, masked_score)


def local(
    layer_input,
    document_lengths,
    attn_gain,
    w_query,
    w_key,
    w_value,
    query_gain,
    key_gain,
    w_out,
    mlp_gain,
    w_gate,
    w_up,
    w_down,
    output_cotangent,
):
    shard_rows = layer_input.shape[2]
    seq_len = shard_rows * lax.axis_size("narrow")
    head_dim = query_gain.shape[0]
    query_cols = w_query.shape[1]
    key_cols = w_key.shape[1]
    query_heads = query_cols // head_dim
    kv_local = key_cols // head_dim
    group_size = query_cols // key_cols
    ff_cols = w_gate.shape[1]
    score_scale = head_dim ** (-0.5)
    w_qkv = jnp.concatenate([w_query, w_key, w_value], axis=1)
    w_both = jnp.concatenate([w_gate, w_up], axis=1)
    attn_gain_f = attn_gain.astype(jnp.float32)
    query_gain_f = query_gain.astype(jnp.float32)
    key_gain_f = key_gain.astype(jnp.float32)
    mlp_gain_f = mlp_gain.astype(jnp.float32)
    totals = None
    small_totals = None
    outputs_list = []
    in_grads = []
    for micro_step in range(layer_input.shape[0]):
        rows_in = layer_input[micro_step, 0].astype(jnp.float32)
        inside, allowed = doc_layout(document_lengths[micro_step, 0], seq_len)
        cos_table, sine_table = rope_tables(inside, head_dim)
        scale_one = rms_scale(rows_in)
        hat_one = rows_in * scale_one
        normed = (hat_one * attn_gain_f).astype(jnp.bfloat16)
        normed_full = lax.all_gather(normed, "narrow", axis=0, tiled=True)
        projected = jnp.dot(normed_full, w_qkv, preferred_element_type=jnp.float32)
        query_raw = projected[:, :query_cols].reshape(seq_len, query_heads, head_dim)
        key_raw = projected[:, query_cols : query_cols + key_cols].reshape(
            seq_len, kv_local, head_dim
        )
        value_rows = (
            projected[:, query_cols + key_cols :]
            .astype(jnp.bfloat16)
            .reshape(seq_len, kv_local, head_dim)
        )
        query_scale = rms_scale(query_raw)
        query_hat = query_raw * query_scale
        query_rot = rotate(query_hat * query_gain_f, cos_table, sine_table).astype(jnp.bfloat16)
        key_scale = rms_scale(key_raw)
        key_hat = key_raw * key_scale
        key_rot = rotate(key_hat * key_gain_f, cos_table, sine_table).astype(jnp.bfloat16)
        grouped = query_rot.reshape(seq_len, kv_local, group_size, head_dim)
        scores = attention_scores(grouped, key_rot, allowed, score_scale)
        top_score = jnp.max(scores, axis=-1, keepdims=True)
        exponent = jnp.exp(scores - top_score)
        total_mass = jnp.sum(exponent, axis=-1, keepdims=True)
        log_mass = top_score + jnp.log(total_mass)
        prob_low = (exponent / total_mass).astype(jnp.bfloat16)
        attn_mix = jnp.einsum(
            "kgtu,ukd->tkgd", prob_low, value_rows, preferred_element_type=jnp.float32
        )
        attn_mix = attn_mix.reshape(seq_len, query_cols).astype(jnp.bfloat16)
        attn_branch = lax.psum_scatter(
            row_product(attn_mix, w_out), "narrow", scatter_dimension=0, tiled=True
        )
        middle = rows_in + attn_branch
        scale_two = rms_scale(middle)
        hat_two = middle * scale_two
        normed_two = (hat_two * mlp_gain_f).astype(jnp.bfloat16)
        normed_two_full = lax.all_gather(normed_two, "narrow", axis=0, tiled=True)
        gate_up = jnp.dot(normed_two_full, w_both, preferred_element_type=jnp.float32)
        gate_pre = gate_up[:, :ff_cols]
        up_proj = gate_up[:, ff_cols:]
        sigmoid_gate = jax.nn.sigmoid(gate_pre)
        silu_gate = gate_pre * sigmoid_gate
        activated = (silu_gate * up_proj).astype(jnp.bfloat16)
        mlp_branch = lax.psum_scatter(
            row_product(activated, w_down).astype(jnp.bfloat16),
            "narrow",
            scatter_dimension=0,
            tiled=True,
        ).astype(jnp.float32)
        outputs_list.append(middle + mlp_branch)
        cot_rows = output_cotangent[micro_step, 0]
        cot_full = lax.all_gather(cot_rows, "narrow", axis=0, tiled=True)
        grad_down = contract_rows(activated, cot_full)
        d_act = contract_cols(cot_full, w_down)
        d_gate = d_act * up_proj * sigmoid_gate * (1.0 + gate_pre * (1.0 - sigmoid_gate))
        d_up = d_act * silu_gate
        d_both = jnp.concatenate([d_gate, d_up], axis=1).astype(jnp.bfloat16)
        grad_both = contract_rows(normed_two_full, d_both)
        d_normed_two = lax.psum_scatter(
            row_back_product(d_both, w_both), "narrow", scatter_dimension=0, tiled=True
        )
        mlp_gain_part = jnp.sum(d_normed_two * hat_two, axis=0)
        d_middle = cot_rows.astype(jnp.float32) + rms_back(
            d_normed_two * mlp_gain_f, hat_two, scale_two
        )
        d_branch = d_middle.astype(jnp.bfloat16)
        d_branch_full = lax.all_gather(d_branch, "narrow", axis=0, tiled=True)
        grad_out = contract_rows(attn_mix, d_branch_full)
        d_mix = contract_cols(d_branch_full, w_out).astype(jnp.bfloat16)
        d_mix = d_mix.reshape(seq_len, kv_local, group_size, head_dim)
        d_prob = jnp.einsum("tkgd,ukd->kgtu", d_mix, value_rows, preferred_element_type=jnp.float32)
        scores_again = attention_scores(grouped, key_rot, allowed, score_scale)
        prob_again = jnp.exp(scores_again - log_mass)
        prob_back_low = prob_again.astype(jnp.bfloat16)
        d_value = jnp.einsum(
            "kgtu,tkgd->ukd", prob_back_low, d_mix, preferred_element_type=jnp.float32
        )
        d_score = prob_again * (d_prob - jnp.sum(prob_again * d_prob, axis=-1, keepdims=True))
        d_score = d_score.astype(jnp.bfloat16)
        d_query = jnp.einsum("kgtu,ukd->tkgd", d_score, key_rot, preferred_element_type=jnp.float32)
        d_query = d_query.reshape(seq_len, query_heads, head_dim) * score_scale
        d_key = (
            jnp.einsum("kgtu,tkgd->ukd", d_score, grouped, preferred_element_type=jnp.float32)
            * score_scale
        )
        d_query_norm = rotate(d_query, cos_table, -sine_table)
        d_key_norm = rotate(d_key, cos_table, -sine_table)
        query_gain_part = jnp.sum(d_query_norm * query_hat, axis=(0, 1))
        key_gain_part = jnp.sum(d_key_norm * key_hat, axis=(0, 1))
        d_query_raw = rms_back(d_query_norm * query_gain_f, query_hat, query_scale)
        d_key_raw = rms_back(d_key_norm * key_gain_f, key_hat, key_scale)
        d_proj = jnp.concatenate(
            [
                d_query_raw.reshape(seq_len, query_cols),
                d_key_raw.reshape(seq_len, key_cols),
                d_value.reshape(seq_len, key_cols),
            ],
            axis=1,
        ).astype(jnp.bfloat16)
        grad_qkv = contract_rows(normed_full, d_proj)
        d_normed = lax.psum_scatter(
            row_back_product(d_proj, w_qkv), "narrow", scatter_dimension=0, tiled=True
        )
        attn_gain_part = jnp.sum(d_normed * hat_one, axis=0)
        in_grads.append(d_middle + rms_back(d_normed * attn_gain_f, hat_one, scale_one))
        grads_now = (grad_qkv, grad_both, grad_out, grad_down)
        small_now = (attn_gain_part, query_gain_part, key_gain_part, mlp_gain_part)
        if totals is None:
            totals = grads_now
            small_totals = small_now
        else:
            totals = tuple((running + extra for running, extra in zip(totals, grads_now)))
            small_totals = tuple(
                (running + extra for running, extra in zip(small_totals, small_now))
            )
    totals = (
        lax.psum_scatter(totals[0], "wide", scatter_dimension=0, tiled=True),
        lax.psum_scatter(totals[1], "wide", scatter_dimension=0, tiled=True),
        lax.psum_scatter(totals[2], "wide", scatter_dimension=1, tiled=True),
        lax.psum_scatter(totals[3], "wide", scatter_dimension=1, tiled=True),
    )
    small_sums = lax.psum(small_totals, ("wide", "narrow"))
    qkv_share, both_share, out_share, down_share = totals
    layer_out = jnp.stack(outputs_list)[:, None]
    in_grad = jnp.stack(in_grads)[:, None]
    return (
        layer_out,
        in_grad,
        small_sums[0],
        qkv_share[:, :query_cols],
        qkv_share[:, query_cols : query_cols + key_cols],
        qkv_share[:, query_cols + key_cols :],
        small_sums[1],
        small_sums[2],
        out_share,
        small_sums[3],
        both_share[:, :ff_cols],
        both_share[:, ff_cols:],
        down_share,
    )


def solution(mesh):
    in_specs = (
        P(None, "wide", "narrow", None),
        P(None, "wide", None),
        P(),
        P(None, "narrow"),
        P(None, "narrow"),
        P(None, "narrow"),
        P(),
        P(),
        P("narrow", None),
        P(),
        P(None, "narrow"),
        P(None, "narrow"),
        P("narrow", None),
        P(None, "wide", "narrow", None),
    )
    out_specs = (
        P(None, "wide", "narrow", None),
        P(None, "wide", "narrow", None),
        P(),
        P("wide", "narrow"),
        P("wide", "narrow"),
        P("wide", "narrow"),
        P(),
        P(),
        P("narrow", "wide"),
        P(),
        P("wide", "narrow"),
        P("wide", "narrow"),
        P("narrow", "wide"),
    )
    return jax.shard_map(local, mesh=mesh, in_specs=in_specs, out_specs=out_specs, check_vma=False)
```

profile of v0, /device:TPU:0, one launch (start us, length us, event | category | flops | bytes accessed | tf_op | source)
XLA Modules:
  0.0 1073.6 jit_solution(3452140487380955168)
XLA Ops:
  9.4 2.1 fusion.34
  18.1 3.2 constant_dynamic-update-slice_fusion.2
  23.4 18.8 %all-gather.11.cloned.1.call-done = bf16[256,2048]{1,0:T(8,128)(2,1)} async-done(((bf16[64,2048]{1,0:T(8,128)(2,1)}), bf16[256,2048]{1,0:T(8,128)(2,1)}) %all-gather.11.cloned.1.call-update) | async-done | bytes 1048592 | tf_op jit(solution)/shard_map/all_gather | solution.py:121
  42.3 3.8 fusion.110
  47.8 24.1 %all-gather.15.cloned.1.call-done = bf16[256,2048]{1,0:T(8,128)(2,1)} async-done(((bf16[64,2048]{1,0:T(8,128)(2,1)}), bf16[256,2048]{1,0:T(8,128)(2,1)}) %all-gather.15.cloned.1.call-update) | async-done | bytes 1048592 | tf_op jit(solution)/shard_map/all_gather | solution.py:121
  71.9 3.8 fusion.113
  82.0 2.2 multiply_multiply_fusion.1
  85.8 1.9 reshape.535
  87.7 2.0 multiply_reduce_fusion.15
  101.0 2.1 fusion.111
  112.0 2.1 fusion.114
  114.8 31.8 %reduce-scatter.13.cloned.1.call-done = f32[64,2048]{1,0:T(8,128)} async-done(((f32[256,2048]{1,0:T(8,128)}), f32[64,2048]{1,0:T(8,128)}) %reduce-scatter.13.cloned.1.call-update) | async-done | bytes 524304 | tf_op jit(solution)/shard_map/reduce_scatter | solution.py:149
  146.6 45.5 %reduce-scatter.17.cloned.1.call-done = f32[64,2048]{1,0:T(8,128)} async-done(((f32[256,2048]{1,0:T(8,128)}), f32[64,2048]{1,0:T(8,128)}) %reduce-scatter.17.cloned.1.call-update) | async-done | bytes 524304 | tf_op jit(solution)/shard_map/reduce_scatter | solution.py:149
  192.1 2.9 multiply_reduce_fusion.10
  196.7 1.9 fusion.107
  198.8 6.0 constant_dynamic-update-slice_fusion.4
  204.8 5.9 constant_dynamic-update-slice_fusion.3
  210.8 13.3 %all-gather.13.cloned.1.call-done = bf16[256,2048]{1,0:T(8,128)(2,1)} async-done(((bf16[64,2048]{1,0:T(8,128)(2,1)}), bf16[256,2048]{1,0:T(8,128)(2,1)}) %all-gather.13.cloned.1.call-update) | async-done | bytes 1048592 | tf_op jit(solution)/shard_map/all_gather | solution.py:156
  224.0 10.0 fusion.112
  234.0 19.5 %all-gather.23.cloned.1.call-done = bf16[1,1,256,2048]{3,2,1,0:T(8,128)(2,1)} async-done(((bf16[1,1,64,2048]{3,2,1,0:T(8,128)(2,1)}), bf16[1,1,256,2048]{3,2,1,0:T(8,128)(2,1)}) %all-gather.23.cloned.1.call-update) | async-done | bytes 1048592 | tf_op jit(solution)/shard_map/all_gather | solution.py:171
  253.5 7.2 multiply_convert_fusion.3
  261.9 9.4 fusion.21
  272.5 42.3 %reduce-scatter.21.cloned.1.call-done = f32[64,2048]{1,0:T(8,128)} async-done(((f32[256,2048]{1,0:T(8,128)}), f32[64,2048]{1,0:T(8,128)}) %reduce-scatter.21.cloned.1.call-update) | async-done | bytes 524304 | tf_op jit(solution)/shard_map/reduce_scatter | solution.py:178
  314.8 2.9 multiply_reduce_fusion.3
  318.9 26.2 %all-gather.17.cloned.1.call-done = bf16[256,2048]{1,0:T(8,128)(2,1)} async-done(((bf16[64,2048]{1,0:T(8,128)(2,1)}), bf16[256,2048]{1,0:T(8,128)(2,1)}) %all-gather.17.cloned.1.call-update) | async-done | bytes 1048592 | tf_op jit(solution)/shard_map/all_gather | solution.py:156
  345.1 10.0 fusion.115
  355.1 19.1 %all-gather.25.cloned.1.call-done = bf16[1,1,256,2048]{3,2,1,0:T(8,128)(2,1)} async-done(((bf16[1,1,64,2048]{3,2,1,0:T(8,128)(2,1)}), bf16[1,1,256,2048]{3,2,1,0:T(8,128)(2,1)}) %all-gather.25.cloned.1.call-update) | async-done | bytes 1048592 | tf_op jit(solution)/shard_map/all_gather | solution.py:171
  374.2 7.2 multiply_convert_fusion.1
  382.6 9.4 fusion.19
  392.1 5.8 convolution_convert_fusion
  399.1 36.4 %reduce-scatter.25.cloned.1.call-done = f32[64,2048]{1,0:T(8,128)} async-done(((f32[256,2048]{1,0:T(8,128)}), f32[64,2048]{1,0:T(8,128)}) %reduce-scatter.25.cloned.1.call-update) | async-done | bytes 524304 | tf_op jit(solution)/shard_map/reduce_scatter | solution.py:178
  435.5 2.0 multiply_reduce_fusion.2
  438.1 26.9 %reduce-scatter.19.cloned.1.call-done = bf16[64,2048]{1,0:T(8,128)(2,1)} async-done(((bf16[256,2048]{1,0:T(8,128)(2,1)}), bf16[64,2048]{1,0:T(8,128)(2,1)}) %reduce-scatter.19.cloned.1.call-update) | async-done | bytes 262160 | tf_op jit(solution)/shard_map/reduce_scatter | solution.py:163
  464.9 2.9 fusion.99
  473.6 21.0 %all-gather.19.cloned.1.call-done = bf16[256,2048]{1,0:T(8,128)(2,1)} async-done(((bf16[64,2048]{1,0:T(8,128)(2,1)}), bf16[256,2048]{1,0:T(8,128)(2,1)}) %all-gather.19.cloned.1.call-update) | async-done | bytes 1048592 | tf_op jit(solution)/shard_map/all_gather | solution.py:186
  494.6 2.7 convolution_convert_fusion.3
  497.3 1.8 copy.291
  499.1 2.3 fusion.10
  501.4 3.3 multiply_reduce_fusion.1
  504.7 19.0 %all-gather.21.cloned.1.call-done = bf16[256,2048]{1,0:T(8,128)(2,1)} async-done(((bf16[64,2048]{1,0:T(8,128)(2,1)}), bf16[256,2048]{1,0:T(8,128)(2,1)}) %all-gather.21.cloned.1.call-update) | async-done | bytes 1048592 | tf_op jit(solution)/shard_map/all_gather | solution.py:186
  523.7 2.7 convolution_convert_fusion.2
  537.8 2.4 multiply_reduce_fusion.13
  544.3 1.9 copy.285
  549.1 4.4 multiply_reduce_fusion.6
  556.5 4.8 fusion.76
  570.8 4.9 fusion.74
  575.8 5.7 convolution_convert_fusion.1
  581.6 2.3 fusion.75
  583.9 4.6 convolution_add_fusion.2
  589.7 11.6 %fusion.20 = f32[2048,3072]{1,0:T(8,128)} fusion(bf16[256,2048]{1,0:T(8,128)(2,1)S(1)} %copy-done.44, bf16[256,1536]{1,0:T(8,128)(2,1)} %copy-done.67, bf16[256,1536]{1,0:T(8,128)(2,1)} %copy-done.66), kind=kOutput, calls=%fused_computation.62 | convolution fusion | flops 3224371200 | bytes 27787264 | tf_op jit(solution)/shard_map/dot_general | solution.py:51
  601.3 16.9 %convolution_add_fusion = f32[2048,3072]{1,0:T(8,128)} fusion(f32[2048,3072]{1,0:T(8,128)} %fusion.20, bf16[256,2048]{1,0:T(8,128)(2,1)S(1)} %copy-done.40, bf16[256,1536]{1,0:T(8,128)(2,1)} %copy-done.64, bf16[256,1536]{1,0:T(8,128)(2,1)S(1)} %copy-done.63), kind=kOutput, calls=%fused_computation | convolution fusion | flops 3230662656 | bytes 52953088 | tf_op jit(solution)/shard_map/dot_general | solution.py:51
  620.3 2.8 convolution_add_fusion.3
  624.3 3.0 fusion.15
  627.3 6.5 convolution_add_fusion.1
  634.6 15.6 %reduce-scatter.27.cloned.1.call-done = f32[64,2048]{1,0:T(8,128)} async-done(((f32[256,2048]{1,0:T(8,128)}), f32[64,2048]{1,0:T(8,128)}) %reduce-scatter.27.cloned.1.call-update) | async-done | bytes 524304 | tf_op jit(solution)/shard_map/reduce_scatter | solution.py:220
  651.9 41.1 %all-reduce = (f32[2048]{0:T(1024)}, f32[128]{0:T(128)}, f32[128]{0:T(128)}, f32[2048]{0:T(1024)}) all-reduce(f32[2048]{0:T(1024)S(1)} %add.226, f32[128]{0:T(128)S(1)} %add.228, f32[128]{0:T(128)S(1)} %add.229, f32[2048]{0:T(1024)S(1)} %add.231), channel_id=1, replica_groups=mesh['wide'=8,'narrow'=4] {'wide','narrow'}, use_global_device_ids=true, to_apply=%region_38.39 | all-reduce | flops 4352 | bytes 34816 | tf_op jit(solution)/shard_map/psum | solution.py:241
  693.1 1.8 fusion.39
  697.4 56.1 %reduce-scatter.29.cloned.1.call-done = f32[256,1024]{1,0:T(8,128)} async-done(((f32[2048,1024]{1,0:T(8,128)}), f32[256,1024]{1,0:T(8,128)}) %reduce-scatter.29.cloned.1.call-update) | async-done | bytes 1048592 | tf_op jit(solution)/shard_map/reduce_scatter | solution.py:236
  753.5 1.9 slice.176
  755.4 2.0 fusion.102
  757.4 157.0 %reduce-scatter.33.cloned.1.call-done = f32[256,3072]{1,0:T(8,128)} async-done(((f32[2048,3072]{1,0:T(8,128)}), f32[256,3072]{1,0:T(8,128)}) %reduce-scatter.33.cloned.1.call-update) | async-done | bytes 3145744 | tf_op jit(solution)/shard_map/reduce_scatter | solution.py:237
  914.3 3.7 fusion.101
  918.1 51.9 %reduce-scatter.31.cloned.1.call-done = f32[512,256]{1,0:T(8,128)} async-done(((f32[512,2048]{1,0:T(8,128)}), f32[512,256]{1,0:T(8,128)}) %reduce-scatter.31.cloned.1.call-update) | async-done | bytes 524304 | tf_op jit(solution)/shard_map/reduce_scatter | solution.py:238
  970.0 96.3 %reduce-scatter.35.cloned.1.call-done = f32[1536,256]{1,0:T(8,128)} async-done(((f32[1536,2048]{1,0:T(8,128)}), f32[1536,256]{1,0:T(8,128)}) %reduce-scatter.35.cloned.1.call-update) | async-done | bytes 1572880 | tf_op jit(solution)/shard_map/reduce_scatter | solution.py:239
  (370 shorter events, 95.4 us)
Async XLA Ops:
  7.2 93.8 %copy-start = (bf16[512,2048]{1,0:T(8,128)(2,1)S(1)}, bf16[512,2048]{1,0:T(8,128)(2,1)}, u32[]{:S(2)}) copy-start(bf16[512,2048]{1,0:T(8,128)(2,1)} %param.22) | copy-start | bytes 6291460
  7.2 35.1 %all-gather.11.cloned.1.call-start = ((), (), s32[]{:S(2)}) async-start(), calls=%async_computation.12 | async-start | bytes 1310720 | tf_op jit(solution)/shard_map/all_gather | solution.py:121
  9.4 11.9 %copy-start.57 = (bf16[2048,256]{1,0:T(8,128)(2,1)S(1)}, bf16[2048,256]{1,0:T(8,128)(2,1)}, u32[]{:S(2)}) copy-start(bf16[2048,256]{1,0:T(8,128)(2,1)} %param.18) | copy-start | bytes 3145732
  11.5 60.4 %all-gather.15.cloned.1.call-start = ((), (), s32[]{:S(2)}) async-start(), calls=%async_computation.16 | async-start | bytes 1310720 | tf_op jit(solution)/shard_map/all_gather | solution.py:121
  12.2 134.4 %reduce-scatter.13.cloned.1.call-start = ((), (), s32[]{:S(2)}) async-start(), calls=%async_computation.13 | async-start | bytes 2621440 | tf_op jit(solution)/shard_map/reduce_scatter | solution.py:149
  13.0 69.0 %copy-start.98 = (f32[128]{0:T(128)}, f32[128]{0:T(128)S(1)}, u32[]{:S(2)}) copy-start(f32[128]{0:T(128)S(1)} %convert_element_type.147) | copy-start | bytes 1540
  15.6 76.6 %copy-start.102 = (f32[128]{0:T(128)}, f32[128]{0:T(128)S(1)}, u32[]{:S(2)}) copy-start(f32[128]{0:T(128)S(1)} %convert_element_type.145) | copy-start | bytes 1540
  46.0 31.4 %copy-start.20 = (f32[256,1024]{1,0:T(8,128)}, f32[256,1024]{1,0:T(8,128)S(1)}, u32[]{:S(2)}) copy-start(f32[256,1024]{1,0:T(8,128)S(1)} %fusion.110) | copy-start | bytes 3145732
  79.3 6.3 copy-start.8
  81.6 6.1 copy-start.10
  85.7 13.0 %copy-start.27 = (bf16[256,4,64]{2,0,1:T(8,128)(2,1)}, bf16[256,4,64]{2,0,1:T(8,128)(2,1)S(1)}, u32[]{:S(2)}) copy-start(bf16[256,4,64]{2,0,1:T(8,128)(2,1)S(1)} %copy.206) | copy-start | bytes 393220
  85.8 13.0 %copy-start.29 = (bf16[256,4,64]{2,0,1:T(8,128)(2,1)}, bf16[256,4,64]{2,0,1:T(8,128)(2,1)S(1)}, u32[]{:S(2)}) copy-start(bf16[256,4,64]{2,0,1:T(8,128)(2,1)S(1)} %copy.205) | copy-start | bytes 393220
  90.6 380.7 %copy-start.83 = (f32[256,2]{0,1:T(2,128)}, f32[256,2]{0,1:T(2,128)S(1)}, u32[]{:S(2)}) copy-start(f32[256,2]{0,1:T(2,128)S(1)} %add_rsqrt_fusion.3) | copy-start | bytes 6148
  103.1 89.0 %reduce-scatter.17.cloned.1.call-start = ((), (), s32[]{:S(2)}) async-start(), calls=%async_computation.17 | async-start | bytes 2621440 | tf_op jit(solution)/shard_map/reduce_scatter | solution.py:149
  103.2 5.3 copy-start.45
  114.1 110.0 %all-gather.13.cloned.1.call-start = ((), (), s32[]{:S(2)}) async-start(), calls=%async_computation.14 | async-start | bytes 1310720 | tf_op jit(solution)/shard_map/all_gather | solution.py:156
  196.6 56.9 %all-gather.23.cloned.1.call-start = ((), (), s32[]{:S(2)}) async-start(), calls=%async_computation.30 | async-start | bytes 1310720 | tf_op jit(solution)/shard_map/all_gather | solution.py:171
  198.6 116.2 %reduce-scatter.21.cloned.1.call-start = ((), (), s32[]{:S(2)}) async-start(), calls=%async_computation.20 | async-start | bytes 2621440 | tf_op jit(solution)/shard_map/reduce_scatter | solution.py:178
  271.2 73.9 %all-gather.17.cloned.1.call-start = ((), (), s32[]{:S(2)}) async-start(), calls=%async_computation.18 | async-start | bytes 1310720 | tf_op jit(solution)/shard_map/all_gather | solution.py:156
  317.7 56.5 %all-gather.25.cloned.1.call-start = ((), (), s32[]{:S(2)}) async-start(), calls=%async_computation.31 | async-start | bytes 1310720 | tf_op jit(solution)/shard_map/all_gather | solution.py:171
  318.4 117.1 %reduce-scatter.25.cloned.1.call-start = ((), (), s32[]{:S(2)}) async-start(), calls=%async_computation.23 | async-start | bytes 2621440 | tf_op jit(solution)/shard_map/reduce_scatter | solution.py:178
  392.0 72.9 %reduce-scatter.19.cloned.1.call-start = ((), (), s32[]{:S(2)}) async-start(), calls=%async_computation.19 | async-start | bytes 1310720 | tf_op jit(solution)/shard_map/reduce_scatter | solution.py:163
  397.9 96.7 %all-gather.19.cloned.1.call-start = ((), (), s32[]{:S(2)}) async-start(), calls=%async_computation.21 | async-start | bytes 1310720 | tf_op jit(solution)/shard_map/all_gather | solution.py:186
  467.9 55.8 %all-gather.21.cloned.1.call-start = ((), (), s32[]{:S(2)}) async-start(), calls=%async_computation.24 | async-start | bytes 1310720 | tf_op jit(solution)/shard_map/all_gather | solution.py:186
  468.6 166.0 %reduce-scatter.23.cloned.1.call-start = ((), (), s32[]{:S(2)}) async-start(), calls=%async_computation.22 | async-start | bytes 2621440 | tf_op jit(solution)/shard_map/reduce_scatter | solution.py:220
  532.3 5.4 copy-start.22
  532.3 5.4 copy-start.23
  532.4 5.4 copy-start.82
  532.8 8.2 copy-start.37
  536.6 5.6 copy-start.38
  543.1 6.0 copy-start.9
  543.1 6.0 copy-start.11
  547.6 5.9 copy-start.76
  549.0 5.2 copy-start.21
  549.1 5.8 copy-start.34
  549.1 6.5 copy-start.86
  556.5 5.9 copy-start.26
  561.3 7.1 copy-start.19
  561.3 7.1 copy-start.59
  561.3 8.6 copy-start.36
  561.3 88.9 %reduce-scatter.27.cloned.1.call-start = ((), (), s32[]{:S(2)}) async-start(), calls=%async_computation.25 | async-start | bytes 2621440 | tf_op jit(solution)/shard_map/reduce_scatter | solution.py:220
  575.7 117.3 %reduce-scatter.15.cloned.1.call-start = ((), (), s32[]{:S(2)}) async-start(), calls=%async_computation.15 | async-start | bytes 1310720 | tf_op jit(solution)/shard_map/reduce_scatter | solution.py:163
  575.8 5.8 copy-start.43
  575.8 5.8 copy-start.69
  581.5 172.0 %reduce-scatter.29.cloned.1.call-start = ((), (), s32[]{:S(2)}) async-start(), calls=%async_computation.26 | async-start | bytes 9437184 | tf_op jit(solution)/shard_map/reduce_scatter | solution.py:236
  588.5 12.8 %copy-start.40 = (bf16[256,2048]{1,0:T(8,128)(2,1)S(1)}, bf16[256,2048]{1,0:T(8,128)(2,1)}, u32[]{:S(2)}) copy-start(bf16[256,2048]{1,0:T(8,128)(2,1)} %all-gather.17.cloned.1.call-done) | copy-start | bytes 3145732
  588.5 12.8 %copy-start.63 = (bf16[256,1536]{1,0:T(8,128)(2,1)S(1)}, bf16[256,1536]{1,0:T(8,128)(2,1)}, u32[]{:S(2)}) copy-start(bf16[256,1536]{1,0:T(8,128)(2,1)} %copy-done.62) | copy-start | bytes 2359300
  588.5 325.8 %reduce-scatter.33.cloned.1.call-start = ((), (), s32[]{:S(2)}) async-start(), calls=%async_computation.28 | async-start | bytes 28311552 | tf_op jit(solution)/shard_map/reduce_scatter | solution.py:237
  618.3 351.7 %reduce-scatter.31.cloned.1.call-start = ((), (), s32[]{:S(2)}) async-start(), calls=%async_computation.27 | async-start | bytes 4718592 | tf_op jit(solution)/shard_map/reduce_scatter | solution.py:238
  623.1 443.2 %reduce-scatter.35.cloned.1.call-start = ((), (), s32[]{:S(2)}) async-start(), calls=%async_computation.29 | async-start | bytes 14155776 | tf_op jit(solution)/shard_map/reduce_scatter | solution.py:239
  633.8 16.4 %copy-start.4 = (bf16[2,1,64,2048]{3,2,1,0:T(8,128)(2,1)S(1)}, bf16[2,1,64,2048]{3,2,1,0:T(8,128)(2,1)}, u32[]{:S(2)}) copy-start(bf16[2,1,64,2048]{3,2,1,0:T(8,128)(2,1)} %param.14) | copy-start | bytes 1572868
  633.8 16.4 %copy-start.79 = (f32[2048]{0:T(1024)S(1)}, f32[2048]{0:T(1024)}, u32[]{:S(2)}) copy-start(f32[2048]{0:T(1024)} %copy-done.78) | copy-start | bytes 24580
  633.8 16.4 %copy-start.91 = (f32[64]{0:T(128)S(1)}, f32[64]{0:T(128)}, u32[]{:S(2)}) copy-start(f32[64]{0:T(128)} %copy-done.90) | copy-start | bytes 772
  633.8 16.4 %copy-start.93 = (f32[64]{0:T(128)S(1)}, f32[64]{0:T(128)}, u32[]{:S(2)}) copy-start(f32[64]{0:T(128)} %copy-done.92) | copy-start | bytes 772
  633.9 59.2 %copy-start.7 = (f32[64,2048]{1,0:T(8,128)S(1)}, f32[64,2048]{1,0:T(8,128)}, u32[]{:S(2)}) copy-start(f32[64,2048]{1,0:T(8,128)} %copy-done.6) | copy-start | bytes 1572868
  633.9 59.2 %copy-start.12 = (bf16[2,1,64,2048]{3,2,1,0:T(8,128)(2,1)S(1)}, bf16[2,1,64,2048]{3,2,1,0:T(8,128)(2,1)}, u32[]{:S(2)}) copy-start(bf16[2,1,64,2048]{3,2,1,0:T(8,128)(2,1)} %param.27) | copy-start | bytes 1572868
  633.9 59.2 %copy-start.15 = (f32[64,2048]{1,0:T(8,128)S(1)}, f32[64,2048]{1,0:T(8,128)}, u32[]{:S(2)}) copy-start(f32[64,2048]{1,0:T(8,128)} %reduce-scatter.21.cloned.1.call-done) | copy-start | bytes 1572868
  633.9 59.2 %copy-start.97 = (f32[64]{0:T(128)S(1)}, f32[64]{0:T(128)}, u32[]{:S(2)}) copy-start(f32[64]{0:T(128)} %copy-done.96) | copy-start | bytes 772
  633.9 59.2 %copy-start.101 = (f32[64]{0:T(128)S(1)}, f32[64]{0:T(128)}, u32[]{:S(2)}) copy-start(f32[64]{0:T(128)} %broadcast_multiply_fusion.7) | copy-start | bytes 772
  651.8 44.1 %copy-start.5 = (f32[64,2048]{1,0:T(8,128)S(1)}, f32[64,2048]{1,0:T(8,128)}, u32[]{:S(2)}) copy-start(f32[64,2048]{1,0:T(8,128)} %get-tuple-element.154) | copy-start | bytes 1572868
  651.9 44.1 %copy-start.14 = (f32[64,2048]{1,0:T(8,128)S(1)}, f32[64,2048]{1,0:T(8,128)}, u32[]{:S(2)}) copy-start(f32[64,2048]{1,0:T(8,128)} %reduce-scatter.25.cloned.1.call-done) | copy-start | bytes 1572868
  651.9 44.1 %copy-start.95 = (f32[64]{0:T(128)S(1)}, f32[64]{0:T(128)}, u32[]{:S(2)}) copy-start(f32[64]{0:T(128)} %add_rsqrt_fusion.4) | copy-start | bytes 772
  651.9 44.1 %copy-start.100 = (f32[64]{0:T(128)S(1)}, f32[64]{0:T(128)}, u32[]{:S(2)}) copy-start(f32[64]{0:T(128)} %broadcast_multiply_fusion.5) | copy-start | bytes 772
  755.4 311.0 %copy-start.1 = (bf16[512,2048]{1,0:T(8,128)(2,1)S(1)}, bf16[512,2048]{1,0:T(8,128)(2,1)}, u32[]{:S(2)}) copy-start(bf16[512,2048]{1,0:T(8,128)(2,1)} %param.22) | copy-start | bytes 6291460
  (60 other events, 140.3 us)
Sparse Core Ops, SparseCore 0:
  11.6 30.6 all-gather.10
  44.4 27.4 all-gather.14
  103.2 43.3 reduce-scatter.12
  148.8 43.1 reduce-scatter.16
  196.8 27.2 all-gather.12
  226.0 27.4 all-gather.22
  271.4 43.3 reduce-scatter.20
  317.8 27.2 all-gather.16
  346.8 27.4 all-gather.24
  392.1 43.3 reduce-scatter.24
  438.4 26.4 reduce-scatter.18
  468.0 26.5 all-gather.18
  496.3 27.4 all-gather.20
  561.4 43.3 reduce-scatter.22
  607.0 43.1 reduce-scatter.26
  653.0 27.1 reduce-scatter.14
  683.5 69.9 reduce-scatter.28
  757.4 156.8 reduce-scatter.32
  918.6 51.3 reduce-scatter.30
  973.9 92.3 reduce-scatter.34
where the time goes:
time: 1080 us; the launch traced here: 1070 us
  waiting for transfers between devices  723 us (67%)
  matrix products  156 us (14%)
  local copies, waits for them, and re-layouts  73.9 us (7%)
  other arithmetic  61.7 us (6%)
  blocking collectives  41.1 us (4%)
  between operations  16.1 us (1%)
    reduce_scatter x1, waiting for transfers between devices, local(): lax.psum_scatter(totals[1], 'wide', scatter_dimension=0, tiled=True)  157 us
    reduce_scatter x1, waiting for transfers between devices, local(): lax.psum_scatter(totals[3], 'wide', scatter_dimension=1, tiled=True)  96.3 us
    reduce_scatter x2, waiting for transfers between devices, local(): lax.psum_scatter(row_back_product(d_both, w_both), 'narrow', scatter_dime...  78.7 us
    reduce_scatter x2, waiting for transfers between devices, local(): lax.psum_scatter(row_product(attn_mix, w_out), 'narrow', scatter_dimensio...  77.3 us
    reduce_scatter x1, waiting for transfers between devices, local(): lax.psum_scatter(totals[0], 'wide', scatter_dimension=0, tiled=True)  56.1 us
    reduce_scatter x1, waiting for transfers between devices, local(): lax.psum_scatter(totals[2], 'wide', scatter_dimension=1, tiled=True)  51.9 us
    dot_general x8, matrix products, contract_rows(): lax.dot_general(left_side, right_side, (((0,), (0,)), ((), ())), preferre...  48.3 us
    dot_general x8, matrix products, contract_cols(): lax.dot_general(left_side, right_side, (((1,), (1,)), ((), ())), preferre...  48.1 us
  transfers between devices with their start and end apart: 20, of which 18 were waited for; matrix products, arithmetic and copies ran while one was open for 16% of the time, Pallas kernels for 0%

commit v1 on v0

--- a/solution.py
+++ b/solution.py
@@ -5,6 +5,19 @@
 
 norm_eps = 1e-06
 masked_score = -1e30
+
+
+def collect(value, axis, dim):
+    size, index, width = (lax.axis_size(axis), lax.axis_index(axis), value.shape[dim])
+    forward = [(i, (i + 1) % size) for i in range(size)]
+    out = jnp.zeros((*value.shape[:dim], size * width, *value.shape[dim + 1 :]), value.dtype)
+    block = value
+    for lap in range(size):
+        owner = (index - lap) % size
+        out = lax.dynamic_update_slice_in_dim(out, block, owner * width, axis=dim)
+        if lap < size - 1:
+            block = lax.ppermute(block, axis, forward)
+    return out
 
 
 def rms_scale(values):
@@ -153,7 +166,7 @@
         scale_two = rms_scale(middle)
         hat_two = middle * scale_two
         normed_two = (hat_two * mlp_gain_f).astype(jnp.bfloat16)
-        normed_two_full = lax.all_gather(normed_two, "narrow", axis=0, tiled=True)
+        normed_two_full = collect(normed_two, "narrow", 0)
         gate_up = jnp.dot(normed_two_full, w_both, preferred_element_type=jnp.float32)
         gate_pre = gate_up[:, :ff_cols]
         up_proj = gate_up[:, ff_cols:]

time: 1080 us -> 1040 us (0.963)
  waiting for transfers between devices: 723 us -> 655 us
  starting transfers between devices: 2.07 us -> 22.4 us
    ppermute x0 -> x6, waiting for transfers between devices: none -> 49 us  [collect(): block = lax.ppermute(block, axis, forward)]
    all_gather x2 -> x0, waiting for transfers between devices: 39.5 us -> none  [local(): normed_two_full = lax.all_gather(normed_two, 'narrow', axis=0, tiled=True)]
    all_gather x2, waiting for transfers between devices: 38.6 us -> 0.01 us  [local(): cot_full = lax.all_gather(cot_rows, 'narrow', axis=0, tiled=True)]
    reduce_scatter x2, waiting for transfers between devices: 78.7 us -> 43 us  [local(): lax.psum_scatter(row_back_product(d_both, w_both), 'narrow', scatter_dime...]
    ppermute x0 -> x6, starting transfers between devices: none -> 21 us  [collect(): block = lax.ppermute(block, axis, forward)]
    unnamed x217 -> x223, local copies, waits for them, and re-layouts: 27.1 us -> 28.4 us
  transfers between devices with their start and end apart: 20 -> 24, of which waited for: 18 -> 19; matrix products, arithmetic and copies ran while one was open for 16% -> 20% of each run, Pallas kernels for 0% -> 0%
where the time goes in v1:
time: 1040 us; the launch traced here: 1030 us
  waiting for transfers between devices  655 us (63%)
  matrix products  156 us (15%)
  local copies, waits for them, and re-layouts  77.2 us (7%)
  other arithmetic  58.2 us (6%)
  blocking collectives  41.1 us (4%)
  starting transfers between devices  22.4 us (2%)
  between operations  16.2 us (2%)
    reduce_scatter x1, waiting for transfers between devices, local(): lax.psum_scatter(totals[1], 'wide', scatter_dimension=0, tiled=True)  157 us
    reduce_scatter x1, waiting for transfers between devices, local(): lax.psum_scatter(totals[3], 'wide', scatter_dimension=1, tiled=True)  96.3 us
    reduce_scatter x2, waiting for transfers between devices, local(): lax.psum_scatter(row_product(attn_mix, w_out), 'narrow', scatter_dimensio...  74.7 us
    reduce_scatter x1, waiting for transfers between devices, local(): lax.psum_scatter(totals[0], 'wide', scatter_dimension=0, tiled=True)  56.1 us
    reduce_scatter x1, waiting for transfers between devices, local(): lax.psum_scatter(totals[2], 'wide', scatter_dimension=1, tiled=True)  51.8 us
    ppermute x6, waiting for transfers between devices, collect(): block = lax.ppermute(block, axis, forward)  49 us
    dot_general x8, matrix products, contract_rows(): lax.dot_general(left_side, right_side, (((0,), (0,)), ((), ())), preferre...  48.4 us
    dot_general x8, matrix products, contract_cols(): lax.dot_general(left_side, right_side, (((1,), (1,)), ((), ())), preferre...  48.2 us
  transfers between devices with their start and end apart: 24, of which 19 were waited for; matrix products, arithmetic and copies ran while one was open for 20% of the time, Pallas kernels for 0%

profile of v1, /device:TPU:0, one launch (start us, length us, event | category | flops | bytes accessed | tf_op | source)
XLA Modules:
  0.0 1025.8 jit_solution(3496927424790119982)
XLA Ops:
  9.4 2.1 fusion.34
  18.1 3.2 constant_dynamic-update-slice_fusion.2
  23.4 18.8 %all-gather.9.cloned.1.call-done = bf16[256,2048]{1,0:T(8,128)(2,1)} async-done(((bf16[64,2048]{1,0:T(8,128)(2,1)}), bf16[256,2048]{1,0:T(8,128)(2,1)}) %all-gather.9.cloned.1.call-update) | async-done | bytes 1048592 | tf_op jit(solution)/shard_map/all_gather | solution.py:134
  42.3 3.8 fusion.110
  47.8 24.1 %all-gather.11.cloned.1.call-done = bf16[256,2048]{1,0:T(8,128)(2,1)} async-done(((bf16[64,2048]{1,0:T(8,128)(2,1)}), bf16[256,2048]{1,0:T(8,128)(2,1)}) %all-gather.11.cloned.1.call-update) | async-done | bytes 1048592 | tf_op jit(solution)/shard_map/all_gather | solution.py:134
  71.9 3.8 fusion.113
  82.9 2.2 multiply_multiply_fusion.1
  91.1 1.9 fusion.72
  100.3 2.1 fusion.111
  111.3 2.1 fusion.114
  113.5 1.9 fusion.107
  116.7 29.2 %reduce-scatter.13.cloned.1.call-done = f32[64,2048]{1,0:T(8,128)} async-done(((f32[256,2048]{1,0:T(8,128)}), f32[64,2048]{1,0:T(8,128)}) %reduce-scatter.13.cloned.1.call-update) | async-done | bytes 524304 | tf_op jit(solution)/shard_map/reduce_scatter | solution.py:162
  145.9 45.5 %reduce-scatter.17.cloned.1.call-done = f32[64,2048]{1,0:T(8,128)} async-done(((f32[256,2048]{1,0:T(8,128)}), f32[64,2048]{1,0:T(8,128)}) %reduce-scatter.17.cloned.1.call-update) | async-done | bytes 524304 | tf_op jit(solution)/shard_map/reduce_scatter | solution.py:162
  191.4 2.9 multiply_reduce_fusion.10
  196.4 6.2 constant_dynamic-update-slice_fusion.4
  202.6 6.2 collective-permute-done
  210.5 3.2 constant_dynamic-update-slice_fusion.3
  214.8 9.3 collective-permute-done.1
  224.1 3.5 collective-permute-start.2
  231.0 3.3 collective-permute-done.2
  235.0 10.2 fusion.112
  245.3 7.2 multiply_convert_fusion.3
  253.7 9.4 fusion.21
  264.5 8.4 collective-permute-done.3
  272.8 6.6 collective-permute-start.4
  279.4 11.3 %collective-permute-done.4 = bf16[64,2048]{1,0:T(8,128)(2,1)S(1)} collective-permute-done((bf16[64,2048]{1,0:T(8,128)(2,1)S(1)}, bf16[64,2048]{1,0:T(8,128)(2,1)S(1)}, u32[]{:S(2)}, u32[]{:S(2)}) %collective-permute-start.4) | collective-permute-done | bytes 262176 | tf_op jit(solution)/shard_map/ppermute | solution.py:19
  290.7 9.1 collective-permute-start.5
  299.9 10.4 %collective-permute-done.5 = bf16[64,2048]{1,0:T(8,128)(2,1)S(1)} collective-permute-done((bf16[64,2048]{1,0:T(8,128)(2,1)S(1)}, bf16[64,2048]{1,0:T(8,128)(2,1)S(1)}, u32[]{:S(2)}, u32[]{:S(2)}) %collective-permute-start.5) | collective-permute-done | bytes 262176 | tf_op jit(solution)/shard_map/ppermute | solution.py:19
  311.3 9.7 fusion.115
  321.0 7.2 multiply_convert_fusion.1
  329.4 9.4 fusion.20
  338.8 5.8 convolution_convert_fusion
  344.7 43.0 %reduce-scatter.25.cloned.1.call-done = f32[64,2048]{1,0:T(8,128)} async-done(((f32[256,2048]{1,0:T(8,128)}), f32[64,2048]{1,0:T(8,128)}) %reduce-scatter.25.cloned.1.call-update) | async-done | bytes 524304 | tf_op jit(solution)/shard_map/reduce_scatter | solution.py:191
  387.7 2.5 multiply_reduce_fusion.3
  391.3 25.8 %reduce-scatter.19.cloned.1.call-done = bf16[64,2048]{1,0:T(8,128)(2,1)} async-done(((bf16[256,2048]{1,0:T(8,128)(2,1)}), bf16[64,2048]{1,0:T(8,128)(2,1)}) %reduce-scatter.19.cloned.1.call-update) | async-done | bytes 262160 | tf_op jit(solution)/shard_map/reduce_scatter | solution.py:176
  417.1 2.9 fusion.99
  425.6 21.1 %all-gather.13.cloned.1.call-done = bf16[256,2048]{1,0:T(8,128)(2,1)} async-done(((bf16[64,2048]{1,0:T(8,128)(2,1)}), bf16[256,2048]{1,0:T(8,128)(2,1)}) %all-gather.13.cloned.1.call-update) | async-done | bytes 1048592 | tf_op jit(solution)/shard_map/all_gather | solution.py:199
  446.8 2.7 convolution_convert_fusion.3
  451.2 2.3 fusion.10
  453.5 3.3 multiply_reduce_fusion.1
  456.8 19.1 %all-gather.15.cloned.1.call-done = bf16[256,2048]{1,0:T(8,128)(2,1)} async-done(((bf16[64,2048]{1,0:T(8,128)(2,1)}), bf16[256,2048]{1,0:T(8,128)(2,1)}) %all-gather.15.cloned.1.call-update) | async-done | bytes 1048592 | tf_op jit(solution)/shard_map/all_gather | solution.py:199
  475.9 2.7 convolution_convert_fusion.2
  489.9 2.4 multiply_reduce_fusion.13
  496.5 1.9 copy.285
  501.3 4.4 multiply_reduce_fusion.6
  508.6 4.8 fusion.76
  523.0 4.8 fusion.74
  528.0 5.7 convolution_convert_fusion.1
  533.8 2.3 fusion.75
  536.1 4.6 convolution_add_fusion.2
  541.9 11.6 %fusion.19 = f32[2048,3072]{1,0:T(8,128)} fusion(bf16[256,2048]{1,0:T(8,128)(2,1)S(1)} %copy-done.15, bf16[256,1536]{1,0:T(8,128)(2,1)} %copy-done.68, bf16[256,1536]{1,0:T(8,128)(2,1)} %copy-done.67), kind=kOutput, calls=%fused_computation.61 | convolution fusion | flops 3224371200 | bytes 27787264 | tf_op jit(solution)/shard_map/dot_general | solution.py:64
  553.5 16.9 %convolution_add_fusion = f32[2048,3072]{1,0:T(8,128)} fusion(f32[2048,3072]{1,0:T(8,128)} %fusion.19, bf16[256,2048]{1,0:T(8,128)(2,1)S(1)} %copy-done.13, bf16[256,1536]{1,0:T(8,128)(2,1)} %copy-done.65, bf16[256,1536]{1,0:T(8,128)(2,1)S(1)} %copy-done.64), kind=kOutput, calls=%fused_computation | convolution fusion | flops 3230662656 | bytes 52953088 | tf_op jit(solution)/shard_map/dot_general | solution.py:64
  572.5 2.8 convolution_add_fusion.3
  576.5 3.0 fusion.15
  579.5 6.5 convolution_add_fusion.1
  586.8 15.7 %reduce-scatter.27.cloned.1.call-done = f32[64,2048]{1,0:T(8,128)} async-done(((f32[256,2048]{1,0:T(8,128)}), f32[64,2048]{1,0:T(8,128)}) %reduce-scatter.27.cloned.1.call-update) | async-done | bytes 524304 | tf_op jit(solution)/shard_map/reduce_scatter | solution.py:233
  604.2 41.1 %all-reduce = (f32[2048]{0:T(1024)}, f32[128]{0:T(128)}, f32[128]{0:T(128)}, f32[2048]{0:T(1024)}) all-reduce(f32[2048]{0:T(1024)S(1)} %add.270, f32[128]{0:T(128)S(1)} %add.272, f32[128]{0:T(128)S(1)} %add.273, f32[2048]{0:T(1024)S(1)} %add.275), channel_id=1, replica_groups=mesh['wide'=8,'narrow'=4] {'wide','narrow'}, use_global_device_ids=true, to_apply=%region_38.39 | all-reduce | flops 4352 | bytes 34816 | tf_op jit(solution)/shard_map/psum | solution.py:254
  649.8 56.1 %reduce-scatter.29.cloned.1.call-done = f32[256,1024]{1,0:T(8,128)} async-done(((f32[2048,1024]{1,0:T(8,128)}), f32[256,1024]{1,0:T(8,128)}) %reduce-scatter.29.cloned.1.call-update) | async-done | bytes 1048592 | tf_op jit(solution)/shard_map/reduce_scatter | solution.py:249
  705.8 1.9 slice.176
  707.7 2.0 fusion.102
  709.7 156.9 %reduce-scatter.33.cloned.1.call-done = f32[256,3072]{1,0:T(8,128)} async-done(((f32[2048,3072]{1,0:T(8,128)}), f32[256,3072]{1,0:T(8,128)}) %reduce-scatter.33.cloned.1.call-update) | async-done | bytes 3145744 | tf_op jit(solution)/shard_map/reduce_scatter | solution.py:250
  866.6 3.7 fusion.101
  870.4 51.8 %reduce-scatter.31.cloned.1.call-done = f32[512,256]{1,0:T(8,128)} async-done(((f32[512,2048]{1,0:T(8,128)}), f32[512,256]{1,0:T(8,128)}) %reduce-scatter.31.cloned.1.call-update) | async-done | bytes 524304 | tf_op jit(solution)/shard_map/reduce_scatter | solution.py:251
  922.2 96.3 %reduce-scatter.35.cloned.1.call-done = f32[1536,256]{1,0:T(8,128)} async-done(((f32[1536,2048]{1,0:T(8,128)}), f32[1536,256]{1,0:T(8,128)}) %reduce-scatter.35.cloned.1.call-update) | async-done | bytes 1572880 | tf_op jit(solution)/shard_map/reduce_scatter | solution.py:252
  (391 shorter events, 107.1 us)
Async XLA Ops:
  7.2 93.1 %copy-start = (bf16[512,2048]{1,0:T(8,128)(2,1)S(1)}, bf16[512,2048]{1,0:T(8,128)(2,1)}, u32[]{:S(2)}) copy-start(bf16[512,2048]{1,0:T(8,128)(2,1)} %param.22) | copy-start | bytes 6291460
  7.2 35.1 %all-gather.9.cloned.1.call-start = ((), (), s32[]{:S(2)}) async-start(), calls=%async_computation.12 | async-start | bytes 1310720 | tf_op jit(solution)/shard_map/all_gather | solution.py:134
  9.4 11.9 %copy-start.58 = (bf16[2048,256]{1,0:T(8,128)(2,1)S(1)}, bf16[2048,256]{1,0:T(8,128)(2,1)}, u32[]{:S(2)}) copy-start(bf16[2048,256]{1,0:T(8,128)(2,1)} %param.18) | copy-start | bytes 3145732
  11.5 60.4 %all-gather.11.cloned.1.call-start = ((), (), s32[]{:S(2)}) async-start(), calls=%async_computation.15 | async-start | bytes 1310720 | tf_op jit(solution)/shard_map/all_gather | solution.py:134
  12.2 133.7 %reduce-scatter.13.cloned.1.call-start = ((), (), s32[]{:S(2)}) async-start(), calls=%async_computation.13 | async-start | bytes 2621440 | tf_op jit(solution)/shard_map/reduce_scatter | solution.py:162
  13.0 69.9 %copy-start.99 = (f32[128]{0:T(128)}, f32[128]{0:T(128)S(1)}, u32[]{:S(2)}) copy-start(f32[128]{0:T(128)S(1)} %convert_element_type.147) | copy-start | bytes 1540
  15.6 75.5 %copy-start.101 = (f32[128]{0:T(128)}, f32[128]{0:T(128)S(1)}, u32[]{:S(2)}) copy-start(f32[128]{0:T(128)S(1)} %convert_element_type.145) | copy-start | bytes 1540
  80.2 6.3 copy-start.8
  82.5 6.6 copy-start.10
  89.5 333.9 %copy-start.84 = (f32[256,2]{0,1:T(2,128)}, f32[256,2]{0,1:T(2,128)S(1)}, u32[]{:S(2)}) copy-start(f32[256,2]{0,1:T(2,128)S(1)} %add_rsqrt_fusion.3) | copy-start | bytes 6148
  102.4 89.0 %reduce-scatter.17.cloned.1.call-start = ((), (), s32[]{:S(2)}) async-start(), calls=%async_computation.16 | async-start | bytes 2621440 | tf_op jit(solution)/shard_map/reduce_scatter | solution.py:162
  113.4 131.9 %all-gather.17.cloned.1.call-start = ((), (), s32[]{:S(2)}) async-start(), calls=%async_computation.28 | async-start | bytes 1310720 | tf_op jit(solution)/shard_map/all_gather | solution.py:184
  115.3 205.7 %all-gather.19.cloned.1.call-start = ((), (), s32[]{:S(2)}) async-start(), calls=%async_computation.29 | async-start | bytes 1310720 | tf_op jit(solution)/shard_map/all_gather | solution.py:184
  115.9 228.8 %reduce-scatter.21.cloned.1.call-start = ((), (), s32[]{:S(2)}) async-start(), calls=%async_computation.18 | async-start | bytes 2621440 | tf_op jit(solution)/shard_map/reduce_scatter | solution.py:191
  196.2 14.3 %slice-start = ((s8[6291456]{0:T(1024)(128)(4,1)}), s8[4194304]{0:T(1024)(128)(4,1)S(1)}, s32[]{:S(2)}) async-start(s8[6291456]{0:T(1024)(128)(4,1)} %bitcast.336), calls=%async_computation.30 | async-start | bytes 8388608
  196.2 14.3 %slice-start.1 = ((s8[6291456]{0:T(1024)(128)(4,1)}), s8[2097152]{0:T(1024)(128)(4,1)S(1)}, s32[]{:S(2)}) async-start(s8[6291456]{0:T(1024)(128)(4,1)} %bitcast.336), calls=%async_computation.31 | async-start | bytes 4194304
  196.2 12.6 %collective-permute-start = (bf16[64,2048]{1,0:T(8,128)(2,1)S(1)}, bf16[64,2048]{1,0:T(8,128)(2,1)}, u32[]{:S(2)}, u32[]{:S(2)}) collective-permute-start(bf16[64,2048]{1,0:T(8,128)(2,1)S(1)} %get-tuple-element.101), channel_id=1, source_target_pairs={{0,1},{1,2},{2,3},{3,0},{4,5},{5,6},{6,7},{7,4},{8,9},{9,10},{10,1... | collective-permute-start | bytes 786440 | tf_op jit(solution)/shard_map/ppermute | solution.py:19
  208.8 15.3 %collective-permute-start.1 = (bf16[64,2048]{1,0:T(8,128)(2,1)}, bf16[64,2048]{1,0:T(8,128)(2,1)}, u32[]{:S(2)}, u32[]{:S(2)}) collective-permute-start(bf16[64,2048]{1,0:T(8,128)(2,1)} %collective-permute-done), channel_id=1, source_target_pairs={{0,1},{1,2},{2,3},{3,0},{4,5},{5,6},{6,7},{7,4},{8,9},{9,10},{10,1... | collective-permute-start | bytes 786440 | tf_op jit(solution)/shard_map/ppermute | solution.py:19
  224.1 10.2 collective-permute-start.2
  263.0 124.6 %reduce-scatter.25.cloned.1.call-start = ((), (), s32[]{:S(2)}) async-start(), calls=%async_computation.21 | async-start | bytes 2621440 | tf_op jit(solution)/shard_map/reduce_scatter | solution.py:191
  264.4 8.5 collective-permute-start.3
  272.8 17.9 %collective-permute-start.4 = (bf16[64,2048]{1,0:T(8,128)(2,1)S(1)}, bf16[64,2048]{1,0:T(8,128)(2,1)S(1)}, u32[]{:S(2)}, u32[]{:S(2)}) collective-permute-start(bf16[64,2048]{1,0:T(8,128)(2,1)S(1)} %collective-permute-done.3), channel_id=1, source_target_pairs={{0,1},{1,2},{2,3},{3,0},{4,5},{5,6},{6,7},{7,4},{8,9},{9,10},{10,1... | collective-permute-start | bytes 786440 | tf_op jit(solution)/shard_map/ppermute | solution.py:19
  290.7 19.5 %collective-permute-start.5 = (bf16[64,2048]{1,0:T(8,128)(2,1)S(1)}, bf16[64,2048]{1,0:T(8,128)(2,1)S(1)}, u32[]{:S(2)}, u32[]{:S(2)}) collective-permute-start(bf16[64,2048]{1,0:T(8,128)(2,1)S(1)} %collective-permute-done.4), channel_id=1, source_target_pairs={{0,1},{1,2},{2,3},{3,0},{4,5},{5,6},{6,7},{7,4},{8,9},{9,10},{10,1... | collective-permute-start | bytes 786440 | tf_op jit(solution)/shard_map/ppermute | solution.py:19
  338.8 78.3 %reduce-scatter.19.cloned.1.call-start = ((), (), s32[]{:S(2)}) async-start(), calls=%async_computation.17 | async-start | bytes 1310720 | tf_op jit(solution)/shard_map/reduce_scatter | solution.py:176
  344.6 102.1 %all-gather.13.cloned.1.call-start = ((), (), s32[]{:S(2)}) async-start(), calls=%async_computation.19 | async-start | bytes 1310720 | tf_op jit(solution)/shard_map/all_gather | solution.py:199
  420.0 55.8 %all-gather.15.cloned.1.call-start = ((), (), s32[]{:S(2)}) async-start(), calls=%async_computation.22 | async-start | bytes 1310720 | tf_op jit(solution)/shard_map/all_gather | solution.py:199
  420.8 166.1 %reduce-scatter.23.cloned.1.call-start = ((), (), s32[]{:S(2)}) async-start(), calls=%async_computation.20 | async-start | bytes 2621440 | tf_op jit(solution)/shard_map/reduce_scatter | solution.py:233
  484.5 5.4 copy-start.26
  484.5 5.4 copy-start.27
  484.9 8.2 copy-start.40
  488.8 5.7 copy-start.41
  495.3 6.0 copy-start.9
  495.3 6.0 copy-start.11
  499.8 5.9 copy-start.77
  501.3 5.8 copy-start.37
  501.3 6.5 copy-start.87
  508.6 5.9 copy-start.30
  513.4 7.1 copy-start.23
  513.4 7.1 copy-start.60
  513.5 8.6 copy-start.39
  513.5 89.0 %reduce-scatter.27.cloned.1.call-start = ((), (), s32[]{:S(2)}) async-start(), calls=%async_computation.23 | async-start | bytes 2621440 | tf_op jit(solution)/shard_map/reduce_scatter | solution.py:233
  527.9 117.5 %reduce-scatter.15.cloned.1.call-start = ((), (), s32[]{:S(2)}) async-start(), calls=%async_computation.14 | async-start | bytes 1310720 | tf_op jit(solution)/shard_map/reduce_scatter | solution.py:176
  527.9 5.8 copy-start.45
  527.9 5.8 copy-start.70
  533.7 172.1 %reduce-scatter.29.cloned.1.call-start = ((), (), s32[]{:S(2)}) async-start(), calls=%async_computation.24 | async-start | bytes 9437184 | tf_op jit(solution)/shard_map/reduce_scatter | solution.py:249
  540.7 12.8 %copy-start.13 = (bf16[256,2048]{1,0:T(8,128)(2,1)S(1)}, bf16[256,2048]{1,0:T(8,128)(2,1)}, u32[]{:S(2)}) copy-start(bf16[256,2048]{1,0:T(8,128)(2,1)} %constant_dynamic-update-slice_fusion.8) | copy-start | bytes 3145732
  540.7 12.8 %copy-start.64 = (bf16[256,1536]{1,0:T(8,128)(2,1)S(1)}, bf16[256,1536]{1,0:T(8,128)(2,1)}, u32[]{:S(2)}) copy-start(bf16[256,1536]{1,0:T(8,128)(2,1)} %copy-done.63) | copy-start | bytes 2359300
  540.7 325.9 %reduce-scatter.33.cloned.1.call-start = ((), (), s32[]{:S(2)}) async-start(), calls=%async_computation.26 | async-start | bytes 28311552 | tf_op jit(solution)/shard_map/reduce_scatter | solution.py:250
  570.5 351.7 %reduce-scatter.31.cloned.1.call-start = ((), (), s32[]{:S(2)}) async-start(), calls=%async_computation.25 | async-start | bytes 4718592 | tf_op jit(solution)/shard_map/reduce_scatter | solution.py:251
  575.3 443.2 %reduce-scatter.35.cloned.1.call-start = ((), (), s32[]{:S(2)}) async-start(), calls=%async_computation.27 | async-start | bytes 14155776 | tf_op jit(solution)/shard_map/reduce_scatter | solution.py:252
  586.0 16.5 %copy-start.7 = (bf16[2,1,64,2048]{3,2,1,0:T(8,128)(2,1)S(1)}, bf16[2,1,64,2048]{3,2,1,0:T(8,128)(2,1)}, u32[]{:S(2)}) copy-start(bf16[2,1,64,2048]{3,2,1,0:T(8,128)(2,1)} %param.14) | copy-start | bytes 1572868
  586.0 16.5 %copy-start.80 = (f32[2048]{0:T(1024)S(1)}, f32[2048]{0:T(1024)}, u32[]{:S(2)}) copy-start(f32[2048]{0:T(1024)} %copy-done.79) | copy-start | bytes 24580
  586.0 16.5 %copy-start.95 = (f32[64]{0:T(128)S(1)}, f32[64]{0:T(128)}, u32[]{:S(2)}) copy-start(f32[64]{0:T(128)} %copy-done.94) | copy-start | bytes 772
  586.0 16.5 %copy-start.97 = (f32[64]{0:T(128)S(1)}, f32[64]{0:T(128)}, u32[]{:S(2)}) copy-start(f32[64]{0:T(128)} %copy-done.96) | copy-start | bytes 772
  586.1 59.3 %copy-start.6 = (f32[64,2048]{1,0:T(8,128)S(1)}, f32[64,2048]{1,0:T(8,128)}, u32[]{:S(2)}) copy-start(f32[64,2048]{1,0:T(8,128)} %copy-done.5) | copy-start | bytes 1572868
  586.1 59.3 %copy-start.16 = (bf16[2,1,64,2048]{3,2,1,0:T(8,128)(2,1)S(1)}, bf16[2,1,64,2048]{3,2,1,0:T(8,128)(2,1)}, u32[]{:S(2)}) copy-start(bf16[2,1,64,2048]{3,2,1,0:T(8,128)(2,1)} %param.27) | copy-start | bytes 1572868
  586.1 59.3 %copy-start.18 = (f32[64,2048]{1,0:T(8,128)S(1)}, f32[64,2048]{1,0:T(8,128)}, u32[]{:S(2)}) copy-start(f32[64,2048]{1,0:T(8,128)} %reduce-scatter.21.cloned.1.call-done) | copy-start | bytes 1572868
  586.1 59.3 %copy-start.92 = (f32[64]{0:T(128)S(1)}, f32[64]{0:T(128)}, u32[]{:S(2)}) copy-start(f32[64]{0:T(128)} %copy-done.91) | copy-start | bytes 772
  586.1 59.3 %copy-start.103 = (f32[64]{0:T(128)S(1)}, f32[64]{0:T(128)}, u32[]{:S(2)}) copy-start(f32[64]{0:T(128)} %broadcast_multiply_fusion.7) | copy-start | bytes 772
  604.1 44.1 %copy-start.4 = (f32[64,2048]{1,0:T(8,128)S(1)}, f32[64,2048]{1,0:T(8,128)}, u32[]{:S(2)}) copy-start(f32[64,2048]{1,0:T(8,128)} %get-tuple-element.158) | copy-start | bytes 1572868
  604.2 44.1 %copy-start.19 = (f32[64,2048]{1,0:T(8,128)S(1)}, f32[64,2048]{1,0:T(8,128)}, u32[]{:S(2)}) copy-start(f32[64,2048]{1,0:T(8,128)} %reduce-scatter.25.cloned.1.call-done) | copy-start | bytes 1572868
  604.2 44.1 %copy-start.93 = (f32[64]{0:T(128)S(1)}, f32[64]{0:T(128)}, u32[]{:S(2)}) copy-start(f32[64]{0:T(128)} %add_rsqrt_fusion.4) | copy-start | bytes 772
  604.2 44.1 %copy-start.102 = (f32[64]{0:T(128)S(1)}, f32[64]{0:T(128)}, u32[]{:S(2)}) copy-start(f32[64]{0:T(128)} %broadcast_multiply_fusion.5) | copy-start | bytes 772
  707.7 310.8 %copy-start.1 = (bf16[512,2048]{1,0:T(8,128)(2,1)S(1)}, bf16[512,2048]{1,0:T(8,128)(2,1)}, u32[]{:S(2)}) copy-start(bf16[512,2048]{1,0:T(8,128)(2,1)} %param.22) | copy-start | bytes 6291460
  (67 other events, 171.0 us)
Sparse Core Ops, SparseCore 0:
  11.6 30.6 all-gather.8
  44.4 27.4 all-gather.10
  102.5 43.3 reduce-scatter.12
  148.2 43.1 reduce-scatter.16
  193.4 36.9 all-gather.16
  231.8 26.1 all-gather.18
  263.2 55.4 reduce-scatter.20
  338.9 48.7 reduce-scatter.24
  390.6 26.4 reduce-scatter.18
  420.2 26.5 all-gather.12
  448.4 27.4 all-gather.14
  513.6 43.3 reduce-scatter.22
  559.3 43.1 reduce-scatter.26
  605.3 27.1 reduce-scatter.14
  635.8 69.9 reduce-scatter.28
  709.7 156.8 reduce-scatter.32
  870.8 51.3 reduce-scatter.30
  926.1 92.3 reduce-scatter.34
